TPU v7x, 32 devices: a whole 2x2x4 slice. The times are simulated.
32 devices in a mesh: dp: 8 (over z, y), mp: 4 (over x, core).
Axes of the slice: x: 2, y: 2, z: 4, core: 2. Of those that a mesh axis runs over, the one named last changes fastest.
Arguments:
- query_inputs: bfloat16 [128, 28672], P(None, 'mp'), may hold values from -0.09375 to 0.09375
- query_grads: bfloat16 [128, 8192], P(None, 'mp'), may hold values from -6 to 6
- basis_inputs: bfloat16 [28672, 28672], P('mp', 'dp'), may hold values from -0.03125 to 0.03125
- basis_grads: bfloat16 [8192, 8192], P('mp', 'dp'), may hold values from -0.0625 to 0.0625
- eig_inputs: float32 [28672], P('dp'), may hold values from 0.25 to 4
- eig_grads: float32 [8192], P('dp'), may hold values from 0.25 to 4
- train_inputs: bfloat16 [6144, 28672], P('dp', 'mp'), may hold values from -0.03540039 to 0.03540039
- train_grads: bfloat16 [6144, 8192], P('dp', 'mp'), may hold values from -0.06591797 to 0.06591797
Outputs:
- scores: float32 [4, 48], P('mp', 'dp')
All inputs are finite; a program needn't handle non-finite values.
Results may differ from a plain program's by a relative error of at most 0.0054.
Values may be sent and summed in bfloat16 or wider, within the bound.
A program may use at most 128 MiB of HBM per device.

v0:
```python
import jax
import jax.numpy as jnp
from jax import lax
from jax.sharding import PartitionSpec as P

LEN = 128
QLEN = 32


def per_device(
    query_inputs,
    query_grads,
    basis_inputs,
    basis_grads,
    eig_inputs,
    eig_grads,
    train_inputs,
    train_grads,
):
    input_cols = basis_inputs.shape[1]
    feat_in = basis_inputs.shape[0]
    row_count = query_inputs.shape[0] // lax.axis_size("mp")
    rot_in = jnp.dot(query_inputs, basis_inputs, preferred_element_type=jnp.float32)
    rot_out = jnp.dot(query_grads, basis_grads, preferred_element_type=jnp.float32)
    rotated = lax.psum_scatter(
        jnp.concatenate([rot_in, rot_out], axis=1), "mp", scatter_dimension=0, tiled=True
    )
    scaled = jnp.concatenate(
        [
            rotated[:, :input_cols] / eig_inputs[None, :],
            rotated[:, input_cols:] / eig_grads[None, :],
        ],
        axis=1,
    ).astype(jnp.bfloat16)
    segment = lax.all_gather(scaled, "mp", axis=0, tiled=True)
    back_in = jnp.einsum(
        "qc,fc->qf", segment[:, :input_cols], basis_inputs, preferred_element_type=jnp.float32
    )
    back_out = jnp.einsum(
        "qc,fc->qf", segment[:, input_cols:], basis_grads, preferred_element_type=jnp.float32
    )
    partial_value = jnp.concatenate([back_in, back_out], axis=1)
    shared_part = lax.psum_scatter(partial_value, "dp", scatter_dimension=0, tiled=True).astype(
        jnp.bfloat16
    )
    directions = lax.all_gather(shared_part, "dp", axis=0, tiled=True)
    train_count = train_inputs.shape[0]
    inner_in = jnp.einsum(
        "qf,tf->qt", directions[:, :feat_in], train_inputs, preferred_element_type=jnp.float32
    )
    inner_out = jnp.einsum(
        "qf,tf->qt", directions[:, feat_in:], train_grads, preferred_element_type=jnp.float32
    )
    pair_sums = lax.psum_scatter(
        jnp.concatenate([inner_in, inner_out], axis=1), "mp", scatter_dimension=0, tiled=True
    )
    products = pair_sums[:, :train_count] * pair_sums[:, train_count:]
    grouped = products.reshape(row_count // QLEN, QLEN, train_count // LEN, LEN)
    return jnp.sum(grouped, axis=(1, 3))


def solution(mesh):
    return jax.shard_map(
        per_device,
        mesh=mesh,
        in_specs=(
            P(None, "mp"),
            P(None, "mp"),
            P("mp", "dp"),
            P("mp", "dp"),
            P("dp"),
            P("dp"),
            P("dp", "mp"),
            P("dp", "mp"),
        ),
        out_specs=P("mp", "dp"),
        check_vma=False,
    )
```

profile of v0, /device:TPU:0, one launch (start us, length us, event | category | flops | bytes accessed | tf_op | source)
XLA Modules:
  0.0 314.6 jit_solution(5288105056165067332)
XLA Ops:
  6.5 0.0 copy-start
  6.5 0.0 reduce-scatter.4.cloned.1.call-start
  6.5 4.0 %fusion.12 = f32[128,1024]{1,0:T(8,128)} fusion(bf16[128,2048]{1,0:T(8,128)(2,1)} %param.9, bf16[2048,1024]{1,0:T(8,128)(2,1)} %param.11), kind=kOutput, calls=%fused_computation.20 | convolution fusion | flops 536870912 | bytes 5242880 | tf_op jit(solution)/shard_map/dot_general | solution.py:24
  10.6 20.9 %fusion.11 = f32[128,3584]{1,0:T(8,128)} fusion(bf16[128,7168]{1,0:T(8,128)(2,1)} %param.8, bf16[7168,3584]{1,0:T(8,128)(2,1)} %param.10), kind=kOutput, calls=%fused_computation.19 | convolution fusion | flops 6576668672 | bytes 55050240 | tf_op jit(solution)/shard_map/dot_general | solution.py:23
  31.5 3.3 %pad_maximum_fusion.1 = f32[128,4608]{1,0:T(8,128)} fusion(f32[128,1024]{1,0:T(8,128)} %fusion.12, f32[128,3584]{1,0:T(8,128)} %fusion.11), kind=kLoop, calls=%fused_computation.1 | loop fusion | flops 589824 | bytes 4718592 | tf_op jit(solution)/shard_map/concatenate | solution.py:26
  34.7 0.0 reduce-scatter.4.cloned.1.call-update
  34.8 0.0 all-gather.3.cloned.1.call-start
  34.8 35.6 %reduce-scatter.4.cloned.1.call-done = f32[32,4608]{1,0:T(8,128)} async-done(((f32[128,4608]{1,0:T(8,128)}), f32[32,4608]{1,0:T(8,128)}) %reduce-scatter.4.cloned.1.call-update) | async-done | bytes 589840 | tf_op jit(solution)/shard_map/reduce_scatter | solution.py:25
  70.4 0.0 copy-done.3
  70.5 0.9 fusion.9
  71.4 1.1 fusion.6
  72.4 0.7 pad_maximum_fusion.3
  73.2 0.0 all-gather.3.cloned.1.call-update
  73.2 0.0 reduce-scatter.6.cloned.1.call-start
  73.3 17.5 %all-gather.3.cloned.1.call-done = bf16[128,4608]{1,0:T(8,128)(2,1)} async-done(((bf16[32,4608]{1,0:T(8,128)(2,1)}), bf16[128,4608]{1,0:T(8,128)(2,1)}) %all-gather.3.cloned.1.call-update) | async-done | bytes 1179664 | tf_op jit(solution)/shard_map/all_gather | solution.py:35
  90.8 4.8 %fusion.7 = f32[128,2048]{1,0:T(8,128)} fusion(bf16[2048,1024]{1,0:T(8,128)(2,1)} %param.11, bf16[128,4608]{1,0:T(8,128)(2,1)} %all-gather.3.cloned.1.call-done), kind=kOutput, calls=%fused_computation.12 | convolution fusion | flops 536870912 | bytes 5505024 | tf_op jit(solution)/shard_map/qc,fc->qf/dot_general | solution.py:39
  95.6 23.4 %fusion.2 = f32[128,7168]{1,0:T(8,128)} fusion(bf16[7168,3584]{1,0:T(8,128)(2,1)} %param.10, bf16[128,4608]{1,0:T(8,128)(2,1)} %all-gather.3.cloned.1.call-done), kind=kOutput, calls=%fused_computation.4 | convolution fusion | flops 6576668672 | bytes 55967744 | tf_op jit(solution)/shard_map/qc,fc->qf/dot_general | solution.py:36
  119.0 4.9 %pad_maximum_fusion = f32[128,9216]{1,0:T(8,128)} fusion(f32[128,2048]{1,0:T(8,128)} %fusion.7, f32[128,7168]{1,0:T(8,128)} %fusion.2), kind=kLoop, calls=%fused_computation | loop fusion | flops 1179648 | bytes 9437184 | tf_op jit(solution)/shard_map/concatenate | solution.py:42
  123.9 0.0 reduce-scatter.6.cloned.1.call-update
  124.0 0.0 all-gather.5.cloned.1.call-start
  124.0 95.8 %reduce-scatter.6.cloned.1.call-done = f32[16,9216]{1,0:T(8,128)} async-done(((f32[128,9216]{1,0:T(8,128)}), f32[16,9216]{1,0:T(8,128)}) %reduce-scatter.6.cloned.1.call-update) | async-done | bytes 589840 | tf_op jit(solution)/shard_map/reduce_scatter | solution.py:43
  219.8 1.8 convert_element_type.4
  221.6 0.0 all-gather.5.cloned.1.call-update
  221.6 0.0 reduce-scatter.8.cloned.1.call-start
  221.7 51.6 %all-gather.5.cloned.1.call-done = bf16[128,9216]{1,0:T(8,128)(2,1)} async-done(((bf16[16,9216]{1,0:T(8,128)(2,1)}), bf16[128,9216]{1,0:T(8,128)(2,1)}) %all-gather.5.cloned.1.call-update) | async-done | bytes 2359312 | tf_op jit(solution)/shard_map/all_gather | solution.py:46
  273.3 2.4 fusion.4
  275.7 7.9 %fusion = f32[128,768]{1,0:T(8,128)S(1)} fusion(bf16[768,7168]{1,0:T(8,128)(2,1)} %param.14, bf16[128,9216]{1,0:T(8,128)(2,1)S(1)} %copy-done.1), kind=kOutput, calls=%fused_computation.2 | convolution fusion | flops 1409286144 | bytes 13238272 | tf_op jit(solution)/shard_map/qf,tf->qt/dot_general | solution.py:48
  283.6 1.0 pad_maximum_fusion.2
  284.5 0.0 reduce-scatter.8.cloned.1.call-update
  284.6 21.9 %reduce-scatter.8.cloned.1.call-done = f32[32,1536]{1,0:T(8,128)} async-done(((f32[128,1536]{1,0:T(8,128)}), f32[32,1536]{1,0:T(8,128)}) %reduce-scatter.8.cloned.1.call-update) | async-done | bytes 196624 | tf_op jit(solution)/shard_map/reduce_scatter | solution.py:54
  306.4 1.0 fusion.10
  307.4 0.6 bitcast_reduce_fusion
  (6 shorter events, 0.0 us)
Async XLA Ops:
  6.5 266.8 %copy-start = (bf16[768,2048]{1,0:T(8,128)(2,1)S(1)}, bf16[768,2048]{1,0:T(8,128)(2,1)}, u32[]{:S(2)}) copy-start(bf16[768,2048]{1,0:T(8,128)(2,1)} %param.15) | copy-start | bytes 9437188
  6.5 63.9 %reduce-scatter.4.cloned.1.call-start = ((), (), s32[]{:S(2)}) async-start(), calls=%async_computation.3 | async-start | bytes 2949120 | tf_op jit(solution)/shard_map/reduce_scatter | solution.py:25
  31.5 39.0 %copy-start.3 = (f32[1024]{0:T(1024)S(1)}, f32[1024]{0:T(1024)}, u32[]{:S(2)}) copy-start(f32[1024]{0:T(1024)} %param.13) | copy-start | bytes 12292
  31.5 39.9 %copy-start.2 = (f32[3584]{0:T(1024)S(1)}, f32[3584]{0:T(1024)}, u32[]{:S(2)}) copy-start(f32[3584]{0:T(1024)} %param.12) | copy-start | bytes 43012
  34.8 56.0 %all-gather.3.cloned.1.call-start = ((), (), s32[]{:S(2)}) async-start(), calls=%async_computation.4 | async-start | bytes 1474560 | tf_op jit(solution)/shard_map/all_gather | solution.py:35
  73.2 146.6 %reduce-scatter.6.cloned.1.call-start = ((), (), s32[]{:S(2)}) async-start(), calls=%async_computation.5 | async-start | bytes 5308416 | tf_op jit(solution)/shard_map/reduce_scatter | solution.py:43
  124.0 149.3 %all-gather.5.cloned.1.call-start = ((), (), s32[]{:S(2)}) async-start(), calls=%async_computation.6 | async-start | bytes 2654208 | tf_op jit(solution)/shard_map/all_gather | solution.py:46
  221.6 84.8 %reduce-scatter.8.cloned.1.call-start = ((), (), s32[]{:S(2)}) async-start(), calls=%async_computation.7 | async-start | bytes 983040 | tf_op jit(solution)/shard_map/reduce_scatter | solution.py:54
  273.3 2.4 copy-start.1
Sparse Core Ops, SparseCore 0:
  34.9 35.5 reduce-scatter.3
  73.3 17.4 all-gather.2
  124.1 95.6 reduce-scatter.5
  221.8 51.4 all-gather.4
  284.7 21.7 reduce-scatter.7
where the time goes:
time: 315 us
  waiting for transfers between devices  223 us (71%)
  matrix products  63.3 us (20%)
  other arithmetic  15.3 us (5%)
  between operations  13.2 us (4%)
    reduce_scatter x1, waiting for transfers between devices, per_device(): lax.psum_scatter(partial_value, 'dp', scatter_dimension=0, tiled=True)  95.8 us
    all_gather x1, waiting for transfers between devices, per_device(): directions = lax.all_gather(shared_part, 'dp', axis=0, tiled=True)  51.6 us
    reduce_scatter x1, waiting for transfers between devices, per_device(): lax.psum_scatter(jnp.concatenate([rot_in, rot_out], axis=1), 'mp', scatte...  35.6 us
    dot_general x1, matrix products, per_device(): jnp.einsum('qc,fc->qf', segment[:, :input_cols], basis_inputs, preferred_...  23.4 us
    reduce_scatter x1, waiting for transfers between devices, per_device(): lax.psum_scatter(jnp.concatenate([inner_in, inner_out], axis=1), 'mp', sc...  21.9 us
    dot_general x1, matrix products, per_device(): jnp.dot(query_inputs, basis_inputs, preferred_element_type=jnp.float32)  20.9 us
    all_gather x1, waiting for transfers between devices, per_device(): segment = lax.all_gather(scaled, 'mp', axis=0, tiled=True)  17.5 us
    dot_general x1, matrix products, per_device(): jnp.einsum('qf,tf->qt', directions[:, :feat_in], train_inputs, preferred_...  7.86 us
  transfers between devices with their start and end apart: 5, of which 5 were waited for; matrix products, arithmetic and copies ran while one was open for 0% of the time, Pallas kernels for 0%

commit v1 on v0

v1 whole, which is shorter than its diff:
```python
import functools
import math

import jax
import jax.numpy as jnp
from jax import lax
from jax.experimental import pallas as pl
from jax.experimental.pallas import tpu as pltpu
from jax.sharding import PartitionSpec as P

LEN = 128
QLEN = 32
WSLOTS = 4
TSLOTS = 3
F32 = jnp.float32
BF16 = jnp.bfloat16
NT = (((1,), (1,)), ((), ()))


def bit_count(size):
    return size.bit_length() - 1


def reverse_bits(value, bits):
    out = 0
    for _ in range(bits):
        out, value = out * 2 + value % 2, value // 2
    return out


def kernel(
    dims,
    qin, qout, ein, eout, bin_, bout, tin, tout,
    out,
    w, tr, acc1, rb1, scaled, acc2, sb2, rb2, pre, inner, rbc,
    wsem, tsem, s1, r1, s2, r2, sc, rc,
):
    rows, fc, cc, tokens, n_in, n_out, dp, mp = dims
    nd, nm = bit_count(dp), bit_count(mp)
    chunks = n_out + n_in
    d, m = lax.axis_index("dp"), lax.axis_index("mp")
    pending = []

    def bit_of(axis, b):
        return lax.rem((d if axis == "dp" else m) // (2**b), 2)

    def partner(axis, b):
        return {axis: (d if axis == "dp" else m) + 2**b * (1 - 2 * bit_of(axis, b))}

    def hint(x, size):
        return pl.multiple_of(x, size)

    def remote(src, dst, ssem, rsem, axis, b):
        copy = pltpu.make_async_remote_copy(
            src_ref=src, dst_ref=dst, send_sem=ssem, recv_sem=rsem,
            device_id=partner(axis, b), device_id_type=pl.DeviceIdType.MESH,
        )
        copy.start()
        pending.append(copy)
        return copy

    def tile_copies(t):
        slot = t % WSLOTS
        c = t % chunks
        base, local, count = (bout, c, n_out) if c < n_out else (bin_, c - n_out, n_in)
        if t < chunks:
            return [
                pltpu.make_async_copy(
                    base.at[:, pl.ds(local * cc, cc)],
                    w.at[slot, pl.ds(0, count * fc)],
                    wsem.at[slot, 0],
                )
            ]
        return [
            pltpu.make_async_copy(
                base.at[pl.ds(local * fc, fc), pl.ds(k * cc, cc)],
                w.at[slot, pl.ds(k * fc, fc)],
                wsem.at[slot, k],
            )
            for k in range(count)
        ]

    def tile_start(t):
        if t < 2 * chunks:
            for copy in tile_copies(t):
                copy.start()

    def tile_wait(t):
        for copy in tile_copies(t):
            copy.wait()

    def train_copy(c):
        base, local = (tout, c) if c < n_out else (tin, c - n_out)
        return pltpu.make_async_copy(
            base.at[:, pl.ds(local * fc, fc)], tr.at[c % TSLOTS], tsem.at[c % TSLOTS]
        )

    for t in range(WSLOTS):
        tile_start(t)

    barrier = pltpu.get_barrier_semaphore()
    for axis, bits in (("dp", nd), ("mp", nm)):
        for b in range(bits):
            pl.semaphore_signal(
                barrier, inc=1, device_id=partner(axis, b),
                device_id_type=pl.DeviceIdType.MESH,
            )
    pl.semaphore_wait(barrier, nd + nm)

    for c in range(min(TSLOTS, chunks)):
        train_copy(c).start()

    def rotate(c):
        slot = c % WSLOTS
        tile_wait(c)
        lhs, count = (qout, n_out) if c < n_out else (qin, n_in)
        acc1[c] = jnp.zeros((rows, cc), F32)

        def step(k, carry):
            at = pl.ds(hint(k * fc, fc), fc)
            acc1[c] += jnp.dot(lhs[:, at], w[slot, at, :], preferred_element_type=F32)
            return carry

        lax.fori_loop(0, count, step, 0)
        tile_start(c + WSLOTS)

    def first(c):
        rotate(c)
        yield
        lo, size, trail = 0, rows, []
        off = 0
        for k in range(nm):
            half = size // 2
            bit = bit_of("mp", k)
            give = hint(lo + (1 - bit) * half, half)
            trail.append(lo)
            copy = remote(
                acc1.at[c, pl.ds(give, half)], rb1.at[c, pl.ds(off, half)],
                s1.at[c, k], r1.at[c, k], "mp", k,
            )
            lo = hint(lo + bit * half, half)
            size = half
            yield
            copy.wait_recv()
            if k < nm - 1:
                acc1[c, pl.ds(lo, half)] += rb1[c, pl.ds(off, half)]
            else:
                eig, local = (eout, c) if c < n_out else (ein, c - n_out)
                total = acc1[c, pl.ds(lo, half)] + rb1[c, pl.ds(off, half)]
                scaled[c, pl.ds(lo, half)] = (
                    total / eig[:, pl.ds(local * cc, cc)]
                ).astype(BF16)
            off += half
        for k in reversed(range(nm)):
            part = scaled.at[c, pl.ds(lo, size)]
            copy = remote(part, part, s1.at[c, nm + k], r1.at[c, nm + k], "mp", k)
            lo = trail[k] if k == 0 else hint(trail[k], size * 2)
            size *= 2
            yield
            copy.wait_recv()

    def rotate_back(c):
        t = chunks + c
        slot = t % WSLOTS
        tile_wait(t)
        start, count = (0, n_out) if c < n_out else (n_out, n_in)
        acc2[c] = jnp.zeros((rows, fc), F32)

        def step(k, carry):
            acc2[c] += lax.dot_general(
                scaled[start + k], w[slot, pl.ds(hint(k * fc, fc), fc), :], NT,
                preferred_element_type=F32,
            )
            return carry

        lax.fori_loop(0, count, step, 0)
        tile_start(t + WSLOTS)

    def second(c):
        rotate_back(c)
        order = list(range(nd))
        if c % 2 and nd > 1:
            order[0], order[1] = order[1], order[0]
        lo, size, trail = 0, rows, []
        off = 0
        for k, b in enumerate(order):
            half = size // 2
            bit = bit_of("dp", b)
            give = hint(lo + (1 - bit) * half, half)
            trail.append(lo)
            sb2[c, pl.ds(off, half)] = acc2[c, pl.ds(give, half)].astype(BF16)
            copy = remote(
                sb2.at[c, pl.ds(off, half)], rb2.at[c, pl.ds(off, half)],
                s2.at[c, k], r2.at[c, k], "dp", b,
            )
            lo = hint(lo + bit * half, half)
            size = half
            yield
            copy.wait_recv()
            total = acc2[c, pl.ds(lo, half)] + rb2[c, pl.ds(off, half)].astype(F32)
            if k < nd - 1:
                acc2[c, pl.ds(lo, half)] = total
            else:
                pre[c, pl.ds(lo, half)] = total.astype(BF16)
            off += half
        for k in reversed(range(nd)):
            part = pre.at[c, pl.ds(lo, size)]
            copy = remote(part, part, s2.at[c, nd + k], r2.at[c, nd + k], "dp", order[k])
            lo = trail[k] if k == 0 else hint(trail[k], size * 2)
            size *= 2
            yield
            copy.wait_recv()
        train_copy(c).wait()
        found = lax.dot_general(
            pre[c], tr[c % TSLOTS], NT, preferred_element_type=F32
        )
        if c + TSLOTS < chunks:
            train_copy(c + TSLOTS).start()
        side = 0 if c < n_out else 1
        block = rows // mp
        for i in range(mp):
            at = pl.ds(reverse_bits(i, nm) * block, block)
            piece = found[i * block : (i + 1) * block]
            if c == 0 or c == n_out:
                inner[side, at] = piece
            else:
                inner[side, at] += piece

    def third(side):
        lo, size, off = 0, rows, 0
        for k in range(nm):
            half = size // 2
            bit = bit_of("mp", k)
            give = hint(lo + (1 - bit) * half, half)
            copy = remote(
                inner.at[side, pl.ds(give, half)], rbc.at[side, pl.ds(off, half)],
                sc.at[side, k], rc.at[side, k], "mp", k,
            )
            lo = hint(lo + bit * half, half)
            size = half
            yield
            copy.wait_recv()
            inner[side, pl.ds(lo, half)] += rbc[side, pl.ds(off, half)]
            off += half
        result.append(inner[side, pl.ds(lo, size)])

    result = []
    live = []

    def turn(fresh=None):
        if fresh is not None:
            next(fresh)
        for item in list(live):
            if next(item, "done") == "done":
                live.remove(item)
        if fresh is not None:
            live.append(fresh)

    for c in range(chunks):
        turn(first(c))
    early = []
    for c in range(n_out):
        item = second(c)
        turn(item)
        early.append(item)
    while any(item not in early for item in live):
        turn()
    outer = None
    for c in range(n_out, chunks):
        turn(second(c))
        if outer is None and not any(item in live for item in early):
            outer = third(0)
            next(outer)
            live.append(outer)
    while live:
        turn()
        if outer is None and not any(item in live for item in early):
            outer = third(0)
            next(outer)
            live.append(outer)
    for _ in third(1):
        pass
    products = result[0] * result[1]
    block = rows // mp
    cells = lax.broadcasted_iota(jnp.int32, out.shape, 1)
    lines = lax.broadcasted_iota(jnp.int32, out.shape, 0)
    answer = jnp.zeros(out.shape, F32)
    for i in range(block // QLEN):
        for n in range(tokens // LEN):
            part = products[i * QLEN : (i + 1) * QLEN, n * LEN : (n + 1) * LEN]
            value = jnp.sum(jnp.sum(part, axis=0, keepdims=True), axis=1, keepdims=True)
            answer = jnp.where((cells == n) & (lines == i), value, answer)
    out[...] = answer
    for copy in pending:
        copy.wait_send()


def per_device(
    dp, mp,
    query_inputs, query_grads, basis_inputs, basis_grads,
    eig_inputs, eig_grads, train_inputs, train_grads,
):
    rows = query_inputs.shape[0]
    feat_in, cols_in = basis_inputs.shape
    feat_out, cols_out = basis_grads.shape
    tokens = train_inputs.shape[0]
    fc = math.gcd(feat_in, feat_out)
    n_in, n_out = feat_in // fc, feat_out // fc
    cc = cols_in // n_in
    nd, nm = bit_count(dp), bit_count(mp)
    chunks = n_in + n_out
    dims = (rows, fc, cc, tokens, n_in, n_out, dp, mp)
    vmem = pl.BlockSpec(memory_space=pltpu.VMEM)
    hbm = pl.BlockSpec(memory_space=pl.ANY)
    dma = pltpu.SemaphoreType.DMA
    return pl.pallas_call(
        functools.partial(kernel, dims),
        out_shape=jax.ShapeDtypeStruct((rows // mp // QLEN, tokens // LEN), F32),
        in_specs=[vmem] * 4 + [hbm] * 4,
        out_specs=vmem,
        scratch_shapes=[
            pltpu.VMEM((WSLOTS, feat_in, cc), BF16),
            pltpu.VMEM((TSLOTS, tokens, fc), BF16),
            pltpu.VMEM((chunks, rows, cc), F32),
            pltpu.VMEM((chunks, rows - rows // mp, cc), F32),
            pltpu.VMEM((chunks, rows, cc), BF16),
            pltpu.VMEM((chunks, rows, fc), F32),
            pltpu.VMEM((chunks, rows - rows // dp, fc), BF16),
            pltpu.VMEM((chunks, rows - rows // dp, fc), BF16),
            pltpu.VMEM((chunks, rows, fc), BF16),
            pltpu.VMEM((2, rows, tokens), F32),
            pltpu.VMEM((2, rows - rows // mp, tokens), F32),
            dma((WSLOTS, n_in)),
            dma((TSLOTS,)),
            dma((chunks, 2 * nm)),
            dma((chunks, 2 * nm)),
            dma((chunks, 2 * nd)),
            dma((chunks, 2 * nd)),
            dma((2, nm)),
            dma((2, nm)),
        ],
        compiler_params=pltpu.CompilerParams(
            collective_id=0, has_side_effects=True, vmem_limit_bytes=66000000
        ),
    )(
        query_inputs, query_grads, eig_inputs[None, :], eig_grads[None, :],
        basis_inputs, basis_grads, train_inputs, train_grads,
    )


def solution(mesh):
    return jax.shard_map(
        functools.partial(per_device, mesh.shape["dp"], mesh.shape["mp"]),
        mesh=mesh,
        in_specs=(
            P(None, "mp"),
            P(None, "mp"),
            P("mp", "dp"),
            P("mp", "dp"),
            P("dp"),
            P("dp"),
            P("dp", "mp"),
            P("dp", "mp"),
        ),
        out_specs=P("mp", "dp"),
        check_vma=False,
    )
```

time: 315 us -> 130 us (0.41)
  waiting for transfers between devices: 223 us -> 0 us
  Pallas kernels: 0 us -> 127 us
  matrix products: 63.3 us -> 0 us
  other arithmetic: 15.3 us -> 0 us
  between operations: 13.2 us -> 0.01 us
    reduce_scatter x3 -> x0, waiting for transfers between devices: 153 us -> none  [the longest x1 95.8 us: per_device(): lax.psum_scatter(partial_value, 'dp', scatter_dimension=0, tiled=True)]
    pallas_call x0 -> x1, Pallas kernels: none -> 127 us  [per_device(): pl.pallas_call(functools.partial(kernel, dims), out_shape=jax.ShapeDtypeS...]
    all_gather x2 -> x0, waiting for transfers between devices: 69.2 us -> none  [the longest x1 51.6 us: per_device(): directions = lax.all_gather(shared_part, 'dp', axis=0, tiled=True)]
    dot_general x6 -> x0, matrix products: 63.3 us -> none  [the longest x1 23.4 us: per_device(): jnp.einsum('qc,fc->qf', segment[:, :input_cols], basis_inputs, preferred_...]
    concatenate x4 -> x0, other arithmetic: 9.94 us -> none  [the longest x1 4.93 us: per_device(): partial_value = jnp.concatenate([back_in, back_out], axis=1)]
  transfers between devices with their start and end apart: 5 -> 0, of which waited for: 5 -> 0; matrix products, arithmetic and copies ran while one was open for 0% -> 0% of each run, Pallas kernels for 0% -> 0%
where the time goes in v1:
time: 130 us
  Pallas kernels  127 us (98%)
  local copies, waits for them, and re-layouts  2.43 us (2%)
    pallas_call x1, Pallas kernels, per_device(): pl.pallas_call(functools.partial(kernel, dims), out_shape=jax.ShapeDtypeS...  127 us

profile of v1, /device:TPU:0, one launch (start us, length us, event | category | flops | bytes accessed | tf_op | source)
XLA Modules:
  0.0 129.5 jit_solution(3425343572891148966)
XLA Ops:
  0.0 1.3 %broadcast_in_dim.6.ein = f32[1,3584]{1,0:T(1,128)} reshape(f32[3584]{0:T(1024)} %param.12) | data formatting | bytes 28672 | tf_op jit(solution)/shard_map/broadcast_in_dim | solution.py:346
  1.3 127.1 %shard_map.82 = f32[1,6]{1,0:T(1,128)} custom-call(bf16[128,7168]{1,0:T(8,128)(2,1)} %qin.1, bf16[128,2048]{1,0:T(8,128)(2,1)} %qout.1, f32[1,3584]{1,0:T(1,128)} %broadcast_in_dim.6.ein, f32[1,1024]{1,0:T(1,128)} %bitcast.1, bf16[7168,3584]{1,0:T(8,128)(2,1)} %bin_.1, bf16[2048,1024]{1,0:T(8,128)(2,1)} %bout.1, bf16[768,7168]{1,0:T(8,128)(2,1)} %tin.1, ...), custom_call_target="tpu_custom_call" | custom-call | tf_op jit(solution)/shard_map/pallas_call | solution.py:316
  128.4 1.1 copy.10
